TPU v7x, 32 devices: a whole 2x2x4 slice. The times are simulated.
32 devices in a mesh: dp: 8 (over z, x), fsdp: 4 (over y, core).
Axes of the slice: x: 2, y: 2, z: 4, core: 2. Of those that a mesh axis runs over, the one named last changes fastest.
Arguments:
- tokens: bfloat16 [16384, 1024], P(('dp', 'fsdp')), may hold values from -6 to 6
- segment_ids: int32 [16384], P(('dp', 'fsdp')), may hold values from 0 to 16383, as said below
- pad_mask: int32 [16384], P(('dp', 'fsdp')), may hold values 0 or 1
- cotangent: bfloat16 [16384, 1024], P(('dp', 'fsdp')), may hold values from -6 to 6
- w_qkv: bfloat16 [1024, 3072], P(('dp', 'fsdp')), may hold values from -0.1875 to 0.1875
- b_query: bfloat16 [1024], P(('dp', 'fsdp')), may hold values from -3 to 3
- b_value: bfloat16 [1024], P(('dp', 'fsdp')), may hold values from -3 to 3
- w_out: bfloat16 [1024, 1024], P(('dp', 'fsdp')), may hold values from -0.75 to 0.75
- b_out: bfloat16 [1024], P(('dp', 'fsdp')), may hold values from -3 to 3
- gain_attn: bfloat16 [1024], P(('dp', 'fsdp')), may hold values from 0.25 to 1.75
- shift_attn: bfloat16 [1024], P(('dp', 'fsdp')), may hold values from -3 to 3
- w_up: bfloat16 [1024, 4096], P(('dp', 'fsdp')), may hold values from -0.1875 to 0.1875
- b_up: bfloat16 [4096], P(('dp', 'fsdp')), may hold values from -3 to 3
- w_down: bfloat16 [4096, 1024], P(('dp', 'fsdp')), may hold values from -0.09375 to 0.09375
- b_down: bfloat16 [1024], P(('dp', 'fsdp')), may hold values from -3 to 3
- gain_ffn: bfloat16 [1024], P(('dp', 'fsdp')), may hold values from 0.25 to 1.75
- shift_ffn: bfloat16 [1024], P(('dp', 'fsdp')), may hold values from -3 to 3
Outputs:
- layer_output: bfloat16 [16384, 1024], P(('dp', 'fsdp'))
- grad_tokens: float32 [16384, 1024], P(('dp', 'fsdp'))
- grad_w_qkv: float32 [1024, 3072], P(('dp', 'fsdp'))
- grad_b_query: float32 [1024], P(('dp', 'fsdp'))
- grad_b_value: float32 [1024], P(('dp', 'fsdp'))
- grad_w_out: float32 [1024, 1024], P(('dp', 'fsdp'))
- grad_b_out: float32 [1024], P(('dp', 'fsdp'))
- grad_gain_attn: float32 [1024], P(('dp', 'fsdp'))
- grad_shift_attn: float32 [1024], P(('dp', 'fsdp'))
- grad_w_up: float32 [1024, 4096], P(('dp', 'fsdp'))
- grad_b_up: float32 [4096], P(('dp', 'fsdp'))
- grad_w_down: float32 [4096, 1024], P(('dp', 'fsdp'))
- grad_b_down: float32 [1024], P(('dp', 'fsdp'))
- grad_gain_ffn: float32 [1024], P(('dp', 'fsdp'))
- grad_shift_ffn: float32 [1024], P(('dp', 'fsdp'))
Inputs may be any that keep to these rules, and one draw needn't show every extreme that they name: `segment_ids`: each token's id is the index of the first token of its segment; ids never fall along the tokens; tokens with equal ids lie in one aligned block of 256 tokens.
All inputs are finite; a program needn't handle non-finite values. No bound on the sum of `pad_mask` on one device may be relied on, other than what follows from the above.
Results may differ from a plain program's by a relative error of at most 0.012.
Values may be sent and summed in bfloat16 or wider, within the bound.
A program may use at most 192 MiB of HBM per device.

v0:
```python
import jax
import jax.numpy as jnp
from jax import lax
from jax.experimental import pallas as pl
from jax.experimental.pallas import tpu as pltpu
from jax.sharding import PartitionSpec as P

HEADS = 16
BLOCK = 512


NEG_FILL = -1e30
EPSILON = 1e-05


def layer_norm(hidden, gain, shift):
    center = hidden - jnp.mean(hidden, -1, keepdims=True)
    spread = jnp.mean(center * center, -1, keepdims=True)
    return center * lax.rsqrt(spread + EPSILON) * gain + shift


def gelu_exact(values_in):
    return jax.nn.gelu(values_in, approximate=False)


def rows_dot(left, right):
    return lax.dot_general(
        left, right, (((0,), (0,)), ((), ())), preferred_element_type=jnp.float32
    )


def back_dot(left, right):
    return lax.dot_general(
        left, right, (((1,), (1,)), ((), ())), preferred_element_type=jnp.float32
    )


def masked_scores(queries, key_rows, seg_block, pad_block):
    scale = float(queries.shape[-1]) ** (-0.5)
    scores = (
        jnp.einsum("qhd,khd->hqk", queries, key_rows, preferred_element_type=jnp.float32) * scale
    )
    span = seg_block.shape[0]
    diagonal = lax.broadcasted_iota(jnp.int32, (span, span), 0) == lax.broadcasted_iota(
        jnp.int32, (span, span), 1
    )
    allowed = (seg_block[:, None] == seg_block[None, :]) & ((pad_block[None, :] == 1) | diagonal)
    return jnp.where(allowed[None], scores, NEG_FILL)


def attend_forward(pieces):
    queries, key_rows, value_rows, seg_block, pad_block = pieces
    scores = masked_scores(queries, key_rows, seg_block, pad_block)
    row_top = jnp.max(scores, -1, keepdims=True)
    row_total = jnp.sum(jnp.exp(scores - row_top), -1, keepdims=True)
    log_total = row_top + jnp.log(row_total)
    weights = jnp.exp(scores - log_total).astype(jnp.bfloat16)
    context = jnp.einsum("hqk,khd->qhd", weights, value_rows, preferred_element_type=jnp.float32)
    return (context.astype(jnp.bfloat16), log_total)


def attend_backward(pieces):
    queries, key_rows, value_rows, context_grad, log_total, seg_block, pad_block = pieces
    scale = float(queries.shape[-1]) ** (-0.5)
    scores = masked_scores(queries, key_rows, seg_block, pad_block)
    probabilities = jnp.exp(scores - log_total)
    value_grad = jnp.einsum(
        "hqk,qhd->khd",
        probabilities.astype(jnp.bfloat16),
        context_grad,
        preferred_element_type=jnp.float32,
    )
    prob_grad = jnp.einsum(
        "qhd,khd->hqk", context_grad, value_rows, preferred_element_type=jnp.float32
    )
    row_inner = jnp.sum(probabilities * prob_grad, -1, keepdims=True)
    score_grad = (probabilities * (prob_grad - row_inner)).astype(jnp.bfloat16)
    query_grad = (
        jnp.einsum("hqk,khd->qhd", score_grad, key_rows, preferred_element_type=jnp.float32) * scale
    )
    key_grad = (
        jnp.einsum("hqk,qhd->khd", score_grad, queries, preferred_element_type=jnp.float32) * scale
    )
    return (
        query_grad.astype(jnp.bfloat16),
        key_grad.astype(jnp.bfloat16),
        value_grad.astype(jnp.bfloat16),
    )


def body(
    tokens,
    segment_ids,
    pad_mask,
    cotangent,
    w_qkv,
    b_query,
    b_value,
    w_out,
    b_out,
    gain_attn,
    shift_attn,
    w_up,
    b_up,
    w_down,
    b_down,
    gain_ffn,
    shift_ffn,
):
    gathered = (
        lax.all_gather(w_qkv, ("dp", "fsdp"), axis=0, tiled=True),
        lax.all_gather(b_query, ("dp", "fsdp"), axis=0, tiled=True),
        lax.all_gather(b_value, ("dp", "fsdp"), axis=0, tiled=True),
        lax.all_gather(w_out, ("dp", "fsdp"), axis=0, tiled=True),
        lax.all_gather(b_out, ("dp", "fsdp"), axis=0, tiled=True),
        lax.all_gather(gain_attn, ("dp", "fsdp"), axis=0, tiled=True),
        lax.all_gather(shift_attn, ("dp", "fsdp"), axis=0, tiled=True),
        lax.all_gather(w_up, ("dp", "fsdp"), axis=0, tiled=True),
        lax.all_gather(b_up, ("dp", "fsdp"), axis=0, tiled=True),
        lax.all_gather(w_down, ("dp", "fsdp"), axis=0, tiled=True),
        lax.all_gather(b_down, ("dp", "fsdp"), axis=0, tiled=True),
        lax.all_gather(gain_ffn, ("dp", "fsdp"), axis=0, tiled=True),
        lax.all_gather(shift_ffn, ("dp", "fsdp"), axis=0, tiled=True),
    )
    (
        qkv_full,
        query_bias,
        value_bias,
        out_full,
        out_bias,
        gain_one,
        shift_one,
        up_full,
        up_bias,
        down_full,
        down_bias,
        gain_two,
        shift_two,
    ) = gathered
    row_count, model_width = tokens.shape
    head_count = HEADS
    head_dim = model_width // head_count
    block_count = row_count // BLOCK

    def split_heads(array):
        return array.reshape(block_count, BLOCK, head_count, head_dim)

    seg_blocks = segment_ids.reshape(block_count, BLOCK)
    pad_blocks = pad_mask.reshape(block_count, BLOCK)
    projected = jnp.dot(tokens, qkv_full, preferred_element_type=jnp.float32)
    queries = (projected[:, :model_width] + query_bias.astype(jnp.float32)).astype(jnp.bfloat16)
    key_rows = projected[:, model_width : 2 * model_width].astype(jnp.bfloat16)
    value_rows = (projected[:, 2 * model_width :] + value_bias.astype(jnp.float32)).astype(
        jnp.bfloat16
    )
    context, log_totals = lax.map(
        attend_forward,
        (
            split_heads(queries),
            split_heads(key_rows),
            split_heads(value_rows),
            seg_blocks,
            pad_blocks,
        ),
    )
    context = context.reshape(row_count, model_width)
    residual_one = (
        tokens.astype(jnp.float32)
        + jnp.dot(context, out_full, preferred_element_type=jnp.float32)
        + out_bias.astype(jnp.float32)
    )
    normed, norm_one_back = jax.vjp(
        layer_norm, residual_one, gain_one.astype(jnp.float32), shift_one.astype(jnp.float32)
    )
    normed_low = normed.astype(jnp.bfloat16)
    upward = jnp.dot(normed_low, up_full, preferred_element_type=jnp.float32) + up_bias.astype(
        jnp.float32
    )
    active, gelu_back = jax.vjp(gelu_exact, upward)
    active_low = active.astype(jnp.bfloat16)
    residual_two = (
        normed
        + jnp.dot(active_low, down_full, preferred_element_type=jnp.float32)
        + down_bias.astype(jnp.float32)
    )
    result, norm_two_back = jax.vjp(
        layer_norm, residual_two, gain_two.astype(jnp.float32), shift_two.astype(jnp.float32)
    )
    qkv_use, out_use, up_use, down_use = (
        lax.all_gather(w_qkv, ("dp", "fsdp"), axis=0, tiled=True),
        lax.all_gather(w_out, ("dp", "fsdp"), axis=0, tiled=True),
        lax.all_gather(w_up, ("dp", "fsdp"), axis=0, tiled=True),
        lax.all_gather(w_down, ("dp", "fsdp"), axis=0, tiled=True),
    )
    grad_two, grad_gain_two, grad_shift_two = norm_two_back(cotangent.astype(jnp.float32))
    branch_grad = grad_two.astype(jnp.bfloat16)
    grad_down = rows_dot(active_low, branch_grad)
    grad_down_bias = jnp.sum(branch_grad.astype(jnp.float32), 0)
    (up_grad,) = gelu_back(back_dot(branch_grad, down_use))
    up_grad_low = up_grad.astype(jnp.bfloat16)
    grad_up = rows_dot(normed_low, up_grad_low)
    grad_up_bias = jnp.sum(up_grad_low.astype(jnp.float32), 0)
    normed_grad = grad_two + back_dot(up_grad_low, up_use)
    grad_one, grad_gain_one, grad_shift_one = norm_one_back(normed_grad)
    attn_grad = grad_one.astype(jnp.bfloat16)
    grad_out = rows_dot(context, attn_grad)
    grad_out_bias = jnp.sum(attn_grad.astype(jnp.float32), 0)
    context_grad = back_dot(attn_grad, out_use).astype(jnp.bfloat16)
    query_grad, key_grad, value_grad = lax.map(
        attend_backward,
        (
            split_heads(queries),
            split_heads(key_rows),
            split_heads(value_rows),
            split_heads(context_grad),
            log_totals,
            seg_blocks,
            pad_blocks,
        ),
    )
    query_grad = query_grad.reshape(row_count, model_width)
    key_grad = key_grad.reshape(row_count, model_width)
    value_grad = value_grad.reshape(row_count, model_width)
    qkv_grad = jnp.concatenate([query_grad, key_grad, value_grad], axis=1)
    grad_qkv = rows_dot(tokens, qkv_grad)
    grad_query_bias = jnp.sum(query_grad.astype(jnp.float32), 0)
    grad_value_bias = jnp.sum(value_grad.astype(jnp.float32), 0)
    grad_tokens = grad_one + back_dot(qkv_grad, qkv_use)
    every_shard = (
        lax.psum_scatter(grad_qkv, ("dp", "fsdp"), scatter_dimension=0, tiled=True),
        lax.psum_scatter(grad_query_bias, ("dp", "fsdp"), scatter_dimension=0, tiled=True),
        lax.psum_scatter(grad_value_bias, ("dp", "fsdp"), scatter_dimension=0, tiled=True),
        lax.psum_scatter(grad_out, ("dp", "fsdp"), scatter_dimension=0, tiled=True),
        lax.psum_scatter(grad_out_bias, ("dp", "fsdp"), scatter_dimension=0, tiled=True),
        lax.psum_scatter(grad_gain_one, ("dp", "fsdp"), scatter_dimension=0, tiled=True),
        lax.psum_scatter(grad_shift_one, ("dp", "fsdp"), scatter_dimension=0, tiled=True),
        lax.psum_scatter(grad_up, ("dp", "fsdp"), scatter_dimension=0, tiled=True),
        lax.psum_scatter(grad_up_bias, ("dp", "fsdp"), scatter_dimension=0, tiled=True),
        lax.psum_scatter(grad_down, ("dp", "fsdp"), scatter_dimension=0, tiled=True),
        lax.psum_scatter(grad_down_bias, ("dp", "fsdp"), scatter_dimension=0, tiled=True),
        lax.psum_scatter(grad_gain_two, ("dp", "fsdp"), scatter_dimension=0, tiled=True),
        lax.psum_scatter(grad_shift_two, ("dp", "fsdp"), scatter_dimension=0, tiled=True),
    )
    (
        shard_qkv,
        shard_query,
        shard_value,
        shard_out,
        shard_out_bias,
        shard_gain_one,
        shard_shift_one,
        shard_up,
        shard_up_bias,
        shard_down,
        shard_down_bias,
        shard_gain_two,
        shard_shift_two,
    ) = every_shard
    return (
        result.astype(jnp.bfloat16),
        grad_tokens,
        shard_qkv,
        shard_query,
        shard_value,
        shard_out,
        shard_out_bias,
        shard_gain_one,
        shard_shift_one,
        shard_up,
        shard_up_bias,
        shard_down,
        shard_down_bias,
        shard_gain_two,
        shard_shift_two,
    )


LATE = (23, 24,)
FORWARD = (
    123, 124, 100, 101, 102, 103, 104, 105, 106, 107, 108, 109, 110, 111, 112, 113, 114, 115, 116, 117, 118, 119,
    120, 121, 122, 600, 223, 224, 200, 323, 324, 300, 201, 400, 500, 601, 202, 301, 203, 302, 401, 501, 602, 204,
    303, 402, 205, 502, 603, 304, 403, 206, 305, 503, 604, 207, 404, 306, 504, 605, 208, 307, 405, 505, 606, 209,
    308, 406, 506, 607, 608, 407, 309, 210, 609, 507, 408, 211, 610, 508, 409, 310, 212, 611, 509, 311, 213, 612,
    410, 312, 214, 613, 510, 215, 614, 615, 313, 616, 411, 216, 314, 511, 617, 315, 217, 412, 512, 618, 316, 218,
    317, 219, 318, 413, 513, 619, 220, 319, 414, 221, 514, 620, 415, 320, 222, 515, 621, 321, 416, 322, 516, 622,
    417, 423, 517, 523, 418, 518, 623, 419, 519, 420, 424, 520, 624, 421, 524, 422, 521, 522, 625, 626,
)
BACKWARD = (
    2000, 0, 100, 1, 101, 2, 200, 300, 102, 3, 201, 301, 103, 4, 202, 302, 5, 203, 303, 6, 400, 500, 7, 104, 2001,
    2002, 401, 501, 204, 304, 8, 600, 700, 105, 2003, 2004, 205, 305, 9, 601, 701, 402, 502, 2005, 106, 2006, 2007,
    800, 403, 503, 206, 306, 10, 602, 702, 107, 2008, 801, 2009, 207, 404, 603, 703, 504, 307, 11, 108, 2010, 2011,
    802, 405, 505, 208, 308, 604, 704, 12, 109, 2012, 803, 2013, 605, 705, 406, 506, 209, 309, 13, 804, 110, 2014,
    407, 507, 210, 310, 14, 606, 706, 111, 2015, 805, 607, 707, 408, 508, 211, 311, 15, 409, 509, 112, 2016, 806,
    608, 708, 410, 807, 510, 212, 312, 113, 16, 114, 2017, 609, 709, 610, 710, 411, 511, 808, 213, 313, 214, 314,
    115, 17, 2018, 611, 711, 412, 512, 809, 215, 315, 18, 413, 513, 116, 19, 117, 810, 216, 316, 20, 217, 21, 2019,
    612, 712, 414, 514, 811, 2020, 118, 317, 2025, 613, 713, 2026, 2021, 218, 22, 318, 614, 714, 415, 812, 515,
    2027, 119, 2028, 2029, 416, 516, 219, 813, 319, 120, 23, 615, 715, 220, 814, 320, 616, 716, 417, 517, 121, 815,
    2022, 221, 321, 418, 518, 122, 617, 717, 816, 222, 2023, 322, 618, 718, 419, 519, 123, 817, 223, 323, 420, 520,
    619, 719, 2024, 818, 421, 620, 720, 521, 819, 422, 522, 621, 721, 820, 622, 423, 722, 523, 821, 623, 723, 822,
    823,
)
BF = jnp.bfloat16
F32 = jnp.float32
MESH = pl.DeviceIdType.MESH
SPAN = 256
CW = 512
NP, NA, NB, NC, ND = 4, 4, 5, 5, 3
LANES = 128


def nn(left, right):
    return lax.dot_general(left, right, (((1,), (0,)), ((), ())), preferred_element_type=F32)


def nt(left, right):
    return lax.dot_general(left, right, (((1,), (1,)), ((), ())), preferred_element_type=F32)


def loop(count, step):
    def run(index, carry):
        step(index)
        return carry

    lax.fori_loop(0, count, run, 0)


def ds(start, size):
    if isinstance(start, int):
        return pl.ds(start, size)
    return pl.ds(pl.multiple_of(start, size), size)


def wait_for(region, sem):
    pltpu.make_async_copy(region, region, sem).wait()


class Place:
    def __init__(self):
        dp, fs = lax.axis_index("dp"), lax.axis_index("fsdp")
        self.z, self.x = dp // 2, dp % 2
        self.y, self.c = fs // 2, fs % 2

    def device(self, z=None, x=None, y=None, c=None):
        z = self.z if z is None else z
        x = self.x if x is None else x
        y = self.y if y is None else y
        c = self.c if c is None else c
        return (z * 2 + x, y * 2 + c)

    def setup(self):
        z, x, y, c = self.z, self.x, self.y, self.c
        self.x1, self.y1 = x + (1 - c) * (1 - 2 * x), y + c * (1 - 2 * y)
        self.x2, self.y2 = x + c * (1 - 2 * x), y + (1 - c) * (1 - 2 * y)
        self.near = self.device(x=self.x1, y=self.y1)
        self.far = self.device(x=self.x2, y=self.y2)
        self.twin = self.device(c=1 - c)
        self.planes = [(z + d) % 4 for d in (1, 2, 3)]
        self.ups = [self.device(z=plane) for plane in self.planes]
        self.downs = [self.device(z=(z - d + 4) % 4) for d in (1, 2, 3)]


def mega(
    tok_hbm, seg_hbm, pad_hbm, v0, v1, v2, v3, v4, v5, v6, v7, bias_hbm,
    cot_hbm, qkv_hbm, out_hbm, up_hbm, down_hbm,
    lo_hbm, gt_hbm, qkv_g, out_g, up_g, down_g, small_g,
    tokens, seg_row, pad_row, seg_key, lines, bias_in, packed, g_qkv, g_out, g_up, g_down, g_small,
    w_qkv, w_out, w_up, w_down, small, vec, up_bias, tok_t, q_s, k_s, v_s, prob, ctx, ctx_t, hat_s, r_s,
    low, low_t, part, act_t, gelu_d, big, ra, rb, rc, rd, acc, bias_up_g, sg, sra, srb, src, srd,
    ag_zr, ag_r1, ag_r2, ag_rc, ag_own, ag_s0, ag_s1, ag_s2,
    sa_s, sa_r, sb_s, sb_r, sc_s, sc_r, sd_s, sd_r, sm_s, sm_r, loc, inp,
    cred_a, cred_b, cred_c, cred_d,
):
    at = Place()
    at.setup()
    z, x, y, c = at.z, at.x, at.y, at.c
    rows, width = tokens.shape
    ff = up_hbm.shape[1]
    blocks = rows // SPAN
    own, near_i, far_i, both_i = x * 2 + y, at.x1 * 2 + at.y1, at.x2 * 2 + at.y2, (1 - x) * 2 + 1 - y

    def send(src, dst, s, r, device):
        pltpu.make_async_remote_copy(
            src_ref=src, dst_ref=dst, send_sem=s, recv_sem=r, device_id=device, device_id_type=MESH
        ).start()

    pieces = [(packed, small, 0, LANES)]
    for hbm, full, wide in ((qkv_hbm, w_qkv, CW), (out_hbm, w_out, CW), (up_hbm, w_up, CW), (down_hbm, w_down, LANES)):
        pieces += [(hbm, full, start, wide) for start in range(0, hbm.shape[1], wide)]
    count = len(pieces)

    def spot(k, plane, square, core):
        _, full, start, wide = pieces[k]
        return full.at[plane, square, core, :, pl.ds(start, wide)]

    every = slice(None)
    barrier = pltpu.get_barrier_semaphore()
    for peer in [at.near, at.far, at.twin] + at.ups:
        pl.semaphore_signal(barrier, inc=1, device_id=peer, device_id_type=MESH)
    inputs = [(v, lines.at[i]) for i, v in enumerate((v0, v1, v2, v3, v4, v5, v6, v7))]
    inputs += [(bias_hbm, bias_in), (seg_hbm, seg_row), (pad_hbm, pad_row), (tok_hbm, tokens)]
    inputs = [pltpu.make_async_copy(src, dst, inp.at[i]) for i, (src, dst) in enumerate(inputs)]
    for copy in inputs:
        copy.start()
    for copy in inputs[:9]:
        copy.wait()
    place = y * 2 + c
    lane = lax.broadcasted_iota(jnp.int32, (8, LANES), 1)
    line = jnp.concatenate([lines[i].astype(F32) for i in range(8)], 0)
    line = jnp.concatenate([line] * 4, 1)
    line = jnp.where((lane >= place * 32) & (lane < place * 32 + 32), line, jnp.zeros_like(line))
    upper = jnp.broadcast_to(bias_in[...].astype(F32), (8, LANES))
    packed[...] = jnp.concatenate([line, upper], 0).astype(BF)
    pl.semaphore_wait(barrier, 6)

    def post(k, src, dst, peers):
        for peer, sem_s, sem_r in peers:
            send(src, dst, sem_s.at[k], sem_r.at[k], peer)

    def pass_on(k, block, peers):
        post(k, block, block, peers)

    twin = (at.twin, ag_s2, ag_rc)
    to_far, to_near = (at.far, ag_s1, ag_r2), (at.near, ag_s1, ag_r1)
    to_ups = [(peer, ag_s0, ag_zr) for peer in at.ups]
    b_far, b_near = (at.far, ag_s0, ag_r2), (at.near, ag_s0, ag_r1)
    b_ups = [(peer, ag_s1, ag_zr) for peer in at.ups]

    def own_piece(k):
        hbm, _, start, wide = pieces[k]
        return hbm.at[:, pl.ds(start, wide)]

    def gather_1(k):
        block = spot(k, z, own, c)
        post(k, own_piece(k), block, to_ups if k not in LATE else [b_near, b_far, twin])
        pltpu.make_async_copy(own_piece(k), block, ag_own.at[k]).start()

    def gather_2(k):
        if k not in LATE:
            wait_for(spot(k, 0, own, c), ag_own.at[k])
            wait_for(spot(k, slice(0, 3), own, c), ag_zr.at[k])
            pass_on(k, spot(k, every, own, c), [to_near, to_far, twin])
        else:
            wait_for(spot(k, z, near_i, c), ag_r1.at[k])
            pass_on(k, spot(k, z, near_i, c), [b_far, twin])

    def gather_3(k):
        if k not in LATE:
            wait_for(spot(k, every, near_i, c), ag_r1.at[k])
            pass_on(k, spot(k, every, near_i, c), [to_far, twin])
        else:
            wait_for(spot(k, z, own, c), ag_own.at[k])
            wait_for(spot(k, z, slice(0, 2), c), ag_r2.at[k])
            pass_on(k, spot(k, z, every, c), b_ups)
            for square in (far_i, both_i):
                pass_on(k, spot(k, z, square, c), [twin])

    def gather_4(k):
        if k not in LATE:
            wait_for(spot(k, every, slice(0, 2), c), ag_r2.at[k])
            for square in (far_i, both_i):
                pass_on(k, spot(k, every, square, c), [twin])
        else:
            wait_for(spot(k, slice(0, 3), every, c), ag_zr.at[k])
            for plane in at.planes:
                pass_on(k, spot(k, plane, every, c), [twin])

    def gather_5(k):
        wait_for(spot(k, every, every, 0), ag_rc.at[k])

    def gather_end(k):
        wait_for(spot(k, slice(0, 3), every, 0), ag_s1.at[k])
        wait_for(spot(k, slice(0, 3), 0, 0), ag_s0.at[k])
        wait_for(spot(k, every, every, 0), ag_s2.at[k])

    keep = [c * (x * 2 + t) + (1 - c) * (t * 2 + y) for t in (0, 1)]
    away = [c * ((1 - x) * 2 + t) + (1 - c) * (t * 2 + 1 - y) for t in (0, 1)]
    mine = (1 - c) * x + c * y
    total = 24

    def send_a(k):
        p, a = k % NP, k % NA
        if k >= NA:
            pl.semaphore_wait(cred_a, 1)
        for plane in range(4):
            send(part.at[p, plane, :, 1 - c], ra.at[a, plane], sa_s.at[p], sa_r.at[a], at.twin)

    def add_a(k):
        p, a = k % NP, k % NA
        wait_for(ra.at[a], sa_r.at[a])

        def step(plane):
            mix = ra[a, plane].astype(F32) + part[p, plane, :, c].astype(F32)
            ra[a, plane] = mix.astype(BF)

        loop(4, step)
        wait_for(ra.at[a], sa_s.at[p])

    def send_b(k):
        a, b = k % NA, k % NB
        if k >= NB:
            pl.semaphore_wait(cred_b, 1)
        for t in (0, 1):
            send(ra.at[a, :, away[t]], rb.at[b, :, t], sb_s.at[a], sb_r.at[b], at.far)

    def add_b(k):
        a, b = k % NA, k % NB
        wait_for(rb.at[b], sb_r.at[b])

        def step(plane):
            for t in (0, 1):
                mix = rb[b, plane, t].astype(F32) + ra[a, plane, keep[t]].astype(F32)
                rb[b, plane, t] = mix.astype(BF)

        loop(4, step)
        wait_for(rb.at[b], sb_s.at[a])
        if k + NA < total:
            pl.semaphore_signal(cred_a, inc=1, device_id=at.twin, device_id_type=MESH)

    def send_c(k):
        b, cc = k % NB, k % NC
        if k >= NC:
            pl.semaphore_wait(cred_c, 1)
        send(rb.at[b, :, 1 - mine], rc.at[cc], sc_s.at[b], sc_r.at[cc], at.near)

    def add_c(k):
        b, cc = k % NB, k % NC
        wait_for(rc.at[cc], sc_r.at[cc])

        def step(plane):
            mix = rc[cc, plane].astype(F32) + rb[b, plane, mine].astype(F32)
            rc[cc, plane] = mix.astype(BF)

        loop(4, step)
        wait_for(rc.at[cc], sc_s.at[b])
        if k + NB < total:
            pl.semaphore_signal(cred_b, inc=1, device_id=at.far, device_id_type=MESH)

    def send_d(k):
        cc, d = k % NC, k % ND
        for o in range(3):
            if k >= ND:
                pl.semaphore_wait(cred_d.at[o], 1)
            send(rc.at[cc, (z + o + 1) % 4], rd.at[d, o], sd_s.at[cc], sd_r.at[d], at.ups[o])

    def target(k, out=False):
        if k < 8:
            pick = (pl.ds(32 * (k // 2), 32), pl.ds(CW * (k % 2), CW))
        elif k < 16:
            pick = (slice(None), pl.ds(CW * (k - 8), CW))
        elif k < 18:
            pick = (slice(None), pl.ds(CW * (k - 16), CW))
        else:
            pick = (slice(None), pl.ds(CW * (k - 18), CW))
        which = (k >= 8) + (k >= 16) + (k >= 18)
        ref = (g_down, g_up, g_out, g_qkv)[which].at[pick]
        return (ref, (down_g, up_g, out_g, qkv_g)[which].at[pick], 2 + which) if out else ref

    def add_d(k):
        cc, d = k % NC, k % ND
        wait_for(rd.at[d], sd_r.at[d])
        mix = rc[cc, z].astype(F32) + rd[d, 0].astype(F32) + rd[d, 1].astype(F32) + rd[d, 2].astype(F32)
        target(k)[...] = mix
        source, dest, index = target(k, True)
        pltpu.make_async_copy(source, dest, loc.at[index]).start()
        wait_for(rd.at[d], sd_s.at[cc])
        if k + NC < total:
            pl.semaphore_signal(cred_c, inc=1, device_id=at.near, device_id_type=MESH)
        if k + ND < total:
            for o in range(3):
                pl.semaphore_signal(cred_d.at[o], inc=1, device_id=at.downs[o], device_id_type=MESH)

    def flat(ref, n):
        return ref[:, :, :, :, ds(n, SPAN)].reshape(width, SPAN)

    def transpose_rows(src, dst):
        def step(n):
            dst[ds(n * SPAN, SPAN), :] = src[:, ds(n * SPAN, SPAN)].T

        loop(width // SPAN, step)

    def project(part_index):
        which, first = part_index // 2, (part_index % 2) * CW
        dst, row = (q_s, k_s, v_s)[which], (0, None, 1)[which]

        def step(n):
            cols = ds(first + n * SPAN, SPAN)
            value = nn(tokens[...], flat(w_qkv, which * width + first + n * SPAN))
            if row is not None:
                value = value + vec[row:row + 1, cols]
            dst[:, cols] = value.astype(BF)

        loop(CW // SPAN, step)

    heads_wide = LANES // 2

    def split(value, high):
        lane = lax.broadcasted_iota(jnp.int32, value.shape, 1)
        return jnp.where((lane >= heads_wide) if high else (lane < heads_wide), value, jnp.zeros_like(value))

    scale = float(heads_wide) ** (-0.5)
    pairs = width // LANES

    def attend(unit):
        block, pair = unit // pairs, unit % pairs
        r, l = ds(block * SPAN, SPAN), ds(pair * LANES, LANES)
        queries, key_rows, values_t = q_s[r, l], k_s[r, l], v_s[r, l].T
        diagonal = lax.broadcasted_iota(jnp.int32, (SPAN, SPAN), 0) == lax.broadcasted_iota(jnp.int32, (SPAN, SPAN), 1)
        allowed = (seg_key[r, :] == seg_row[:, r].astype(F32)) | diagonal
        halves = []
        for high in (0, 1):
            scores = nt(split(key_rows, high), queries) * scale
            scores = jnp.where(allowed, scores, NEG_FILL)
            raised = jnp.exp(scores - jnp.max(scores, 0, keepdims=True))
            weights = (raised * (1.0 / jnp.sum(raised, 0, keepdims=True))).astype(BF)
            prob[unit, high] = weights
            halves.append(nn(values_t[heads_wide * high:heads_wide * (high + 1), :], weights))
        joined = jnp.concatenate(halves, 0).astype(BF)
        ctx_t[l, r] = joined
        ctx[r, l] = joined.T

    def attend_back(unit):
        block, pair = unit // pairs, unit % pairs
        r, l = ds(block * SPAN, SPAN), ds(pair * LANES, LANES)
        queries, key_rows, values, grads = q_s[r, l], k_s[r, l], v_s[r, l], ctx[r, l]
        keys_t = key_rows.T
        value_grad = jnp.zeros((SPAN, LANES), F32)
        key_grad = jnp.zeros((SPAN, LANES), F32)
        halves = []
        for high in (0, 1):
            weights = prob[unit, high]
            value_grad = value_grad + nn(weights, split(grads, high))
            wide = weights.astype(F32)
            prob_grad = nt(split(values, high), grads)
            inner = jnp.sum(wide * prob_grad, 0, keepdims=True)
            score_grad = (wide * (prob_grad - inner)).astype(BF)
            key_grad = key_grad + nn(score_grad, split(queries, high))
            halves.append(nn(keys_t[heads_wide * high:heads_wide * (high + 1), :], score_grad))
        q_s[r, l] = (jnp.concatenate(halves, 0) * scale).T.astype(BF)
        k_s[r, l] = (key_grad * scale).astype(BF)
        v_s[r, l] = value_grad.astype(BF)

    ROWS = 64

    def folded(value):
        return jnp.sum(value.reshape(ROWS // 8, 8, width), 0)

    def norm_stats(hidden):
        center = hidden - jnp.mean(hidden, -1, keepdims=True)
        spread = jnp.mean(center * center, -1, keepdims=True)
        r = lax.rsqrt(spread + EPSILON)
        return center * r, r

    def out_project():
        def step(n):
            cols = ds(n * SPAN, SPAN)
            big[:, cols] = tokens[:, cols].astype(F32) + nn(ctx[...], flat(w_out, n * SPAN)) + vec[2:3, cols]

        loop(width // SPAN, step)

    def norm_one():
        def step(n):
            r = ds(n * ROWS, ROWS)
            hat, inverse = norm_stats(big[r, :])
            hat_s[r, :] = hat
            r_s[r, :] = inverse
            normed = hat * vec[3:4, :] + vec[4:5, :]
            low[r, :] = normed.astype(BF)
            big[r, :] = normed + vec[5:6, :]

        loop(rows // ROWS, step)

    def up_units(first, count):
        def step(index):
            u = first + index
            cols = ds(u * SPAN, SPAN)
            value = nn(low[...], flat(w_up, u * SPAN)) + up_bias[:, cols]
            phi = 0.5 + 0.5 * lax.erf(value * (0.5 ** 0.5))
            active = (value * phi).astype(BF)
            slope = phi + value * (jnp.exp(-0.5 * value * value) * 0.3989422804014327)
            gelu_d[:, cols] = slope.astype(BF)
            act_t[ds(u * 2, 2)] = active.T.reshape(2, LANES, rows)
            wide = u // 2
            part[wide // 2, ds((wide % 2) * 2, 2), :, :, :, ds((u % 2) * SPAN, SPAN)] = active.reshape(2, 4, 2, 32, SPAN)

        loop(count, step)

    def down_piece(index):
        cols = pl.ds(index * SPAN, SPAN)
        left = jnp.concatenate([part[w // 2, 2 * (w % 2):2 * (w % 2) + 2].reshape(rows, CW) for w in range(ff // CW)], 1)
        big[:, cols] += nn(left, w_down[:, :, :, :, cols].reshape(ff, SPAN))

    def norm_two():
        for row in range(6):
            acc[row] = jnp.zeros((8, width), F32)

        def step(n):
            r = ds(n * ROWS, ROWS)
            hat, inverse = norm_stats(big[r, :])
            cot = ctx[r, :].astype(F32)
            ctx[r, :] = (hat * vec[6:7, :] + vec[7:8, :]).astype(BF)
            acc[0] += folded(cot * hat)
            acc[1] += folded(cot)
            scaled = cot * vec[6:7, :]
            grad = inverse * (
                scaled - jnp.mean(scaled, -1, keepdims=True) - hat * jnp.mean(scaled * hat, -1, keepdims=True)
            )
            big[r, :] = grad
            rounded = grad.astype(BF)
            low[r, :] = rounded
            acc[2] += folded(rounded.astype(F32))

        loop(rows // ROWS, step)

    def norm_one_back():
        def step(n):
            r = ds(n * ROWS, ROWS)
            incoming, hat = big[r, :], hat_s[r, :]
            acc[3] += folded(incoming * hat)
            acc[4] += folded(incoming)
            scaled = incoming * vec[3:4, :]
            grad = r_s[r, :] * (
                scaled - jnp.mean(scaled, -1, keepdims=True) - hat * jnp.mean(scaled * hat, -1, keepdims=True)
            )
            big[r, :] = grad
            rounded = grad.astype(BF)
            low[r, :] = rounded
            acc[5] += folded(rounded.astype(F32))

        loop(rows // ROWS, step)

    def put_part(k, left, right):
        slot = k % NP

        def step(index):
            m, n = index // 2, index % 2
            value = nn(left(m), right(n)).astype(BF).reshape(2, 4, 2, 32, SPAN)
            part[slot, ds(2 * m, 2), :, :, :, ds(n * SPAN, SPAN)] = value

        loop(4, step)

    def produce(k):
        half = lambda ref: lambda m: ref[ds(m * CW, CW), :]
        col = lambda ref, first: lambda n: ref[:, ds(first + n * SPAN, SPAN)]
        if k < 8:
            group = 32 * (k // 2)
            put_part(
                k,
                lambda m: act_t[ds(16 * m, 16), group:group + 32, :].reshape(CW, rows),
                col(low, (k % 2) * CW),
            )
        elif k < 16:
            put_part(k, half(low_t), col(gelu_d, (k - 8) * CW))
        elif k < 18:
            put_part(k, half(ctx_t), col(low, (k - 16) * CW))
        else:
            put_part(k, half(tok_t), col((q_s, k_s, v_s)[(k - 18) // 2], (k % 2) * CW))

    def up_back(first, count):
        def step(index):
            u = first + index
            cols = ds(u * SPAN, SPAN)

            def half(i, total_up):
                r = ds(i * SPAN, SPAN)
                weight = w_down[u // 4, u % 4].reshape(SPAN, width)
                grad = (nt(low[r, :], weight) * gelu_d[r, cols].astype(F32)).astype(BF)
                gelu_d[r, cols] = grad
                return total_up + jnp.sum(grad.astype(F32), 0, keepdims=True)

            bias_up_g[:, cols] = lax.fori_loop(0, blocks, half, jnp.zeros((1, SPAN), F32))

        loop(count, step)

    def normed_back(plane):
        cols = pl.ds(plane * SPAN, SPAN)

        def half(i):
            r = ds(i * SPAN, SPAN)
            big[r, cols] += nt(gelu_d[r, :], w_up[plane].reshape(SPAN, ff))

        loop(blocks, half)

    def context_back():
        def step(plane):
            ctx[:, ds(plane * SPAN, SPAN)] = nt(low[...], w_out[plane].reshape(SPAN, width)).astype(BF)

        loop(4, step)

    def token_back(plane):
        cols = pl.ds(plane * SPAN, SPAN)

        def half(i):
            r = ds(i * SPAN, SPAN)
            weight = w_qkv[plane].reshape(SPAN, 3 * width)
            total_grad = nt(q_s[r, :], weight[:, :width]) + nt(k_s[r, :], weight[:, width:2 * width])
            big[r, cols] += total_grad + nt(v_s[r, :], weight[:, 2 * width:])

        loop(blocks, half)

    def first_rows():
        for copy in inputs[9:]:
            copy.wait()
        for n in range(rows // LANES):
            r = slice(LANES * n, LANES * (n + 1))
            key = jnp.where(pad_row[:, r] == 1, seg_row[:, r], -1).astype(F32)
            seg_key[r, :] = jnp.broadcast_to(key, (LANES, LANES)).T[:, 0:1]
        transpose_rows(tokens, tok_t)

    def unpack():
        for g in range(8):
            tile = small[g // 2, 2 * (g % 2), 0].astype(F32)
            for j in range(1, 4):
                tile = tile + small[g // 2, 2 * (g % 2) + j // 2, j % 2].astype(F32)
            vec[:, LANES * g:LANES * (g + 1)] = tile[0:8]
        for j in range(32):
            up_bias[:, LANES * j:LANES * (j + 1)] = small[j // 8, (j % 8) // 2, j % 2].astype(F32)[8:9]

    def norm_first():
        pltpu.make_async_copy(cot_hbm, ctx, loc.at[0]).start()
        norm_one()

    units = blocks * pairs
    forward = [first_rows, unpack]
    forward += [lambda i=i: project(i) for i in range(6)]
    forward += [lambda i=i: loop(units // 4, lambda u: attend(u + i * (units // 4))) for i in range(4)]
    forward += [out_project, norm_first, lambda: transpose_rows(low, low_t)]
    forward += [lambda i=i: up_units(2 * i, 2) for i in range(8)]
    forward += [lambda i=i: down_piece(i) for i in range(4)]
    gathers = (None, gather_1, gather_2, gather_3, gather_4, gather_5)
    for code in FORWARD:
        if code < 600:
            gathers[code // 100](code % 100)
        else:
            forward[code - 600]()

    pltpu.make_async_copy(cot_hbm, ctx, loc.at[0]).wait()

    def small_grads():
        for row in range(6):
            acc[row, 0:1] = jnp.sum(acc[row], 0, keepdims=True)
        for g in range(8):
            cols = slice(LANES * g, LANES * (g + 1))
            query_sum = jnp.sum(q_s[:, cols].astype(F32), 0, keepdims=True)
            value_sum = jnp.sum(v_s[:, cols].astype(F32), 0, keepdims=True)
            tile = jnp.concatenate(
                [query_sum, value_sum] + [acc[row, 0:1, cols] for row in (5, 3, 4, 2, 0, 1)], 0
            )
            for j in range(4 * g, 4 * g + 4):
                sg[j // 8, (j % 8) // 2, j % 2, 0:8] = tile
                line = bias_up_g[:, LANES * j:LANES * (j + 1)]
                sg[j // 8, (j % 8) // 2, j % 2, 8:16] = jnp.broadcast_to(line, (8, LANES))

    def small_a():
        for plane in range(4):
            send(sg.at[plane, :, 1 - c], sra.at[plane], sm_s.at[0], sm_r.at[0], at.twin)

    def small_b():
        wait_for(sra, sm_r.at[0])
        for plane in range(4):
            sra[plane] += sg[plane, :, c]
        for t in (0, 1):
            send(sra.at[:, away[t]], srb.at[:, t], sm_s.at[1], sm_r.at[1], at.far)

    def small_c():
        wait_for(srb, sm_r.at[1])
        for t in (0, 1):
            srb[:, t] += sra[:, keep[t]]
        send(srb.at[:, 1 - mine], src, sm_s.at[2], sm_r.at[2], at.near)

    def small_d():
        wait_for(src, sm_r.at[2])
        src[...] += srb[:, mine]
        for o in range(3):
            send(src.at[(z + o + 1) % 4], srd.at[o], sm_s.at[3], sm_r.at[3], at.ups[o])

    def small_e():
        wait_for(srd, sm_r.at[3])
        g_small[...] = src[z] + srd[0] + srd[1] + srd[2]
        g_small[0:8] = pltpu.roll(g_small[0:8], (4 - place) % 4 * 32, 1)
        pltpu.make_async_copy(g_small, small_g, loc.at[6]).start()
        wait_for(sra, sm_s.at[0])
        wait_for(srb, sm_s.at[1])
        wait_for(src, sm_s.at[2])
        wait_for(srd, sm_s.at[3])

    def finish_norm():
        norm_two()
        pltpu.make_async_copy(ctx, lo_hbm, loc.at[1]).start()

    def to_context():
        pltpu.make_async_copy(ctx, lo_hbm, loc.at[1]).wait()
        context_back()

    def write_tokens():
        pltpu.make_async_copy(big, gt_hbm, loc.at[0]).start()

    backward = [finish_norm]
    backward += [lambda i=i: up_back(2 * i, 2) for i in range(8)]
    backward += [lambda i=i: normed_back(i) for i in range(4)]
    backward += [norm_one_back, to_context]
    backward += [lambda i=i: loop(units // 4, lambda u: attend_back(u + i * (units // 4))) for i in range(4)]
    backward += [small_grads, small_a, small_b, small_c, small_d, small_e]
    backward += [lambda i=i: token_back(i) for i in range(4)]
    backward += [write_tokens]
    stages = (produce, send_a, add_a, send_b, add_b, send_c, add_c, send_d, add_d)
    for code in BACKWARD:
        if code < 2000:
            stages[code // 100](code % 100)
        else:
            backward[code - 2000]()

    for k in range(count):
        gather_end(k)
    pltpu.make_async_copy(big, gt_hbm, loc.at[0]).wait()
    for index, (source, dest) in enumerate(((g_down, down_g), (g_up, up_g), (g_out, out_g), (g_qkv, qkv_g), (g_small, small_g))):
        pltpu.make_async_copy(source, dest, loc.at[2 + index]).wait()


def finish(
    lo, gt, qkv, out, up, down, small,
    lo_o, gt_o, qkv_o, out_o, up_o, down_o, s0, s1, s2, s3, s4, s5, s6, s7, s8,
    lo_v, gt_v, qkv_v, out_v, up_v, down_v, sem_in, sem_out,
):
    moves = []
    for src, mid, dst, parts in (
        (gt, gt_v, gt_o, 4), (lo, lo_v, lo_o, 2), (up, up_v, up_o, 1), (down, down_v, down_o, 1), (qkv, qkv_v, qkv_o, 1),
        (out, out_v, out_o, 1),
    ):
        size = src.shape[0] // parts
        for i in range(parts):
            r, n = pl.ds(i * size, size), len(moves)
            moves.append((
                pltpu.make_async_copy(src.at[r], mid.at[r], sem_in.at[n]),
                pltpu.make_async_copy(mid.at[r], dst.at[r], sem_out.at[n]),
            ))
    for take, _ in moves:
        take.start()
    for i, ref in enumerate((s0, s1, s2, s3, s4, s5, s6, s7)):
        ref[...] = small[i:i + 1, 0:32]
    s8[...] = small[8:9, :]
    for take, put in moves:
        take.wait()
        put.start()
    for _, put in moves:
        put.wait()


def fused(
    tokens, segment_ids, pad_mask, cotangent, w_qkv, b_query, b_value, w_out, b_out, gain_attn, shift_attn,
    w_up, b_up, w_down, b_down, gain_ffn, shift_ffn,
):
    rows, width = tokens.shape
    ff = w_up.shape[1]
    vectors = [b_query, b_value, b_out, gain_attn, shift_attn, b_down, gain_ffn, shift_ffn]
    vectors = [v.reshape(1, v.shape[0]) for v in vectors] + [b_up.reshape(1, LANES)]
    vmem = pl.BlockSpec(memory_space=pltpu.VMEM)
    anyw = pl.BlockSpec(memory_space=pl.ANY)
    pairs = width // LANES
    blocks = rows // SPAN
    count = 25
    dma = pltpu.SemaphoreType.DMA
    own_shapes = [w.shape for w in (w_qkv, w_out, w_up, w_down)]
    scratch = [
        pltpu.VMEM((rows, width), BF),
        pltpu.VMEM((1, rows), jnp.int32),
        pltpu.VMEM((1, rows), jnp.int32),
        pltpu.VMEM((rows, 1), F32),
        pltpu.VMEM((8, 1, 32), BF),
        pltpu.VMEM((1, LANES), BF),
        pltpu.VMEM((16, LANES), BF),
    ]
    scratch += [pltpu.VMEM(shape, F32) for shape in own_shapes] + [pltpu.VMEM((16, LANES), F32)]
    scratch += [
        pltpu.VMEM((4, 4, 2, 32, 3 * width), BF),
        pltpu.VMEM((4, 4, 2, 32, width), BF),
        pltpu.VMEM((4, 4, 2, 32, ff), BF),
        pltpu.VMEM((4, 4, 2, 128, width), BF),
        pltpu.VMEM((4, 4, 2, 16, LANES), BF),
        pltpu.VMEM((8, width), F32),
        pltpu.VMEM((1, ff), F32),
        pltpu.VMEM((width, rows), BF),
        pltpu.VMEM((rows, width), BF),
        pltpu.VMEM((rows, width), BF),
        pltpu.VMEM((rows, width), BF),
        pltpu.VMEM((blocks * pairs, 2, SPAN, SPAN), BF),
        pltpu.VMEM((rows, width), BF),
        pltpu.VMEM((width, rows), BF),
        pltpu.VMEM((rows, width), F32),
        pltpu.VMEM((rows, 1), F32),
        pltpu.VMEM((rows, width), BF),
        pltpu.VMEM((width, rows), BF),
        pltpu.VMEM((NP, 4, 4, 2, 32, CW), BF),
        pltpu.VMEM((ff // LANES, LANES, rows), BF),
        pltpu.VMEM((rows, ff), BF),
        pltpu.VMEM((rows, width), F32),
        pltpu.VMEM((NA, 4, 4, 32, CW), BF),
        pltpu.VMEM((NB, 4, 2, 32, CW), BF),
        pltpu.VMEM((NC, 4, 32, CW), BF),
        pltpu.VMEM((ND, 3, 32, CW), BF),
        pltpu.VMEM((6, 8, width), F32),
        pltpu.VMEM((1, ff), F32),
        pltpu.VMEM((4, 4, 2, 16, LANES), F32),
        pltpu.VMEM((4, 4, 16, LANES), F32),
        pltpu.VMEM((4, 2, 16, LANES), F32),
        pltpu.VMEM((4, 16, LANES), F32),
        pltpu.VMEM((3, 16, LANES), F32),
    ]
    scratch += [dma((count,))] * 8
    scratch += [
        dma((NP,)), dma((NA,)), dma((NA,)), dma((NB,)), dma((NB,)), dma((NC,)), dma((NC,)), dma((ND,)),
        dma((4,)), dma((4,)), dma((7,)), dma((12,)),
        pltpu.SemaphoreType.REGULAR, pltpu.SemaphoreType.REGULAR, pltpu.SemaphoreType.REGULAR,
        pltpu.SemaphoreType.REGULAR((3,)),
    ]
    result, grad_tokens, g_qkv, g_out, g_up, g_down, g_small = pl.pallas_call(
        mega,
        out_shape=(
            jax.ShapeDtypeStruct((rows, width), BF),
            jax.ShapeDtypeStruct((rows, width), F32),
            jax.ShapeDtypeStruct(w_qkv.shape, F32),
            jax.ShapeDtypeStruct(w_out.shape, F32),
            jax.ShapeDtypeStruct(w_up.shape, F32),
            jax.ShapeDtypeStruct(w_down.shape, F32),
            jax.ShapeDtypeStruct((16, LANES), F32),
        ),
        in_specs=[anyw] * 17,
        out_specs=[anyw] * 7,
        scratch_shapes=scratch,
        compiler_params=pltpu.CompilerParams(
            collective_id=0, has_side_effects=True, vmem_limit_bytes=67043328
        ),
        name="layer",
    )(
        tokens, segment_ids.reshape(1, rows), pad_mask.reshape(1, rows), *vectors, cotangent, w_qkv, w_out, w_up, w_down
    )
    arrays = (result, grad_tokens, g_qkv, g_out, g_up, g_down)
    moved = pl.pallas_call(
        finish,
        out_shape=[jax.ShapeDtypeStruct(a.shape, a.dtype) for a in arrays]
        + [jax.ShapeDtypeStruct((1, 32), F32)] * 8 + [jax.ShapeDtypeStruct((1, LANES), F32)],
        in_specs=[anyw] * 6 + [vmem],
        out_specs=[anyw] * 6 + [vmem] * 9,
        scratch_shapes=[pltpu.VMEM(a.shape, a.dtype) for a in arrays] + [dma((10,))] * 2,
        compiler_params=pltpu.CompilerParams(vmem_limit_bytes=67043328),
        name="finish",
    )(*arrays, g_small)
    result, grad_tokens, g_qkv, g_out, g_up, g_down = moved[:6]
    own = [m.reshape(m.shape[1]) for m in moved[6:]]
    return (
        result, grad_tokens, g_qkv, own[0], own[1], g_out, own[2], own[3], own[4], g_up, own[8], g_down,
        own[5], own[6], own[7],
    )


def layer(*arrays):
    fast = lax.axis_size("dp") == 8 and lax.axis_size("fsdp") == 4
    return fused(*arrays) if fast else body(*arrays)


def solution(mesh):
    placed = (
        P(("dp", "fsdp"), None),
        P(("dp", "fsdp")),
        P(("dp", "fsdp")),
        P(("dp", "fsdp"), None),
        P(("dp", "fsdp"), None),
        P(("dp", "fsdp")),
        P(("dp", "fsdp")),
        P(("dp", "fsdp"), None),
        P(("dp", "fsdp")),
        P(("dp", "fsdp")),
        P(("dp", "fsdp")),
        P(("dp", "fsdp"), None),
        P(("dp", "fsdp")),
        P(("dp", "fsdp"), None),
        P(("dp", "fsdp")),
        P(("dp", "fsdp")),
        P(("dp", "fsdp")),
    )
    return jax.shard_map(
        layer,
        mesh=mesh,
        in_specs=placed,
        out_specs=(
            P(("dp", "fsdp"), None),
            P(("dp", "fsdp"), None),
            P(("dp", "fsdp"), None),
            P(("dp", "fsdp")),
            P(("dp", "fsdp")),
            P(("dp", "fsdp"), None),
            P(("dp", "fsdp")),
            P(("dp", "fsdp")),
            P(("dp", "fsdp")),
            P(("dp", "fsdp"), None),
            P(("dp", "fsdp")),
            P(("dp", "fsdp"), None),
            P(("dp", "fsdp")),
            P(("dp", "fsdp")),
            P(("dp", "fsdp")),
        ),
        check_vma=False,
    )
```

profile of v0, /device:TPU:0, one launch (start us, length us, event | category | flops | bytes accessed | tf_op | source)
XLA Modules:
  0.0 246.1 jit_solution(16237431799375027426)
XLA Ops:
  0.7 240.0 %layer.1 = (bf16[512,1024]{1,0:T(8,128)(2,1)}, f32[512,1024]{1,0:T(8,128)}, f32[32,3072]{1,0:T(8,128)}, f32[32,1024]{1,0:T(8,128)}, f32[32,4096]{1,0:T(8,128)}, /*index=5*/f32[128,1024]{1,0:T(8,128)}, f32[16,128]{1,0:T(8,128)}) custom-call(bf16[512,1024]{1,0:T(8,128)(2,1)} %tok_hbm.1, s32[1,512]{1,0:T(1,128)} %bitcast.20, s32[1,512]{1,0:T(1,128)} %bitcast.21, ...), custom_call_target="tpu_custom_call" | custom-call | tf_op jit(solution)/shard_map/layer/pallas_call | solution.py:1015
  240.7 5.3 %finish.1 = (bf16[512,1024]{1,0:T(8,128)(2,1)}, f32[512,1024]{1,0:T(8,128)}, f32[32,3072]{1,0:T(8,128)}, f32[32,1024]{1,0:T(8,128)}, f32[32,4096]{1,0:T(8,128)},...) custom-call(bf16[512,1024]{1,0:T(8,128)(2,1)} %get-tuple-element.37., ...), custom_call_target="tpu_custom_call" | custom-call | tf_op jit(solution)/shard_map/finish/pallas_call | solution.py:1037
where the time goes:
time: 246 us
  Pallas kernels  245 us (100%)
    pallas_call x1, Pallas kernels, fused(): pl.pallas_call(mega, out_shape=(jax.ShapeDtypeStruct((rows, width), BF),...  240 us
    pallas_call x1, Pallas kernels, fused(): pl.pallas_call(finish, out_shape=[jax.ShapeDtypeStruct(a.shape, a.dtype)...  5.26 us

commit v1 on v0

--- a/solution.py
+++ b/solution.py
@@ -276,6 +276,7 @@
 
 
 LATE = (23, 24,)
+ZFIRST = (1, 3,)
 FORWARD = (
     123, 124, 100, 101, 102, 103, 104, 105, 106, 107, 108, 109, 110, 111, 112, 113, 114, 115, 116, 117, 118, 119,
     120, 121, 122, 600, 223, 224, 200, 323, 324, 300, 201, 400, 500, 601, 202, 301, 203, 302, 401, 501, 602, 204,
@@ -286,18 +287,18 @@
     417, 423, 517, 523, 418, 518, 623, 419, 519, 420, 424, 520, 624, 421, 524, 422, 521, 522, 625, 626,
 )
 BACKWARD = (
-    2000, 0, 100, 1, 101, 2, 200, 300, 102, 3, 201, 301, 103, 4, 202, 302, 5, 203, 303, 6, 400, 500, 7, 104, 2001,
-    2002, 401, 501, 204, 304, 8, 600, 700, 105, 2003, 2004, 205, 305, 9, 601, 701, 402, 502, 2005, 106, 2006, 2007,
-    800, 403, 503, 206, 306, 10, 602, 702, 107, 2008, 801, 2009, 207, 404, 603, 703, 504, 307, 11, 108, 2010, 2011,
-    802, 405, 505, 208, 308, 604, 704, 12, 109, 2012, 803, 2013, 605, 705, 406, 506, 209, 309, 13, 804, 110, 2014,
-    407, 507, 210, 310, 14, 606, 706, 111, 2015, 805, 607, 707, 408, 508, 211, 311, 15, 409, 509, 112, 2016, 806,
-    608, 708, 410, 807, 510, 212, 312, 113, 16, 114, 2017, 609, 709, 610, 710, 411, 511, 808, 213, 313, 214, 314,
-    115, 17, 2018, 611, 711, 412, 512, 809, 215, 315, 18, 413, 513, 116, 19, 117, 810, 216, 316, 20, 217, 21, 2019,
-    612, 712, 414, 514, 811, 2020, 118, 317, 2025, 613, 713, 2026, 2021, 218, 22, 318, 614, 714, 415, 812, 515,
-    2027, 119, 2028, 2029, 416, 516, 219, 813, 319, 120, 23, 615, 715, 220, 814, 320, 616, 716, 417, 517, 121, 815,
-    2022, 221, 321, 418, 518, 122, 617, 717, 816, 222, 2023, 322, 618, 718, 419, 519, 123, 817, 223, 323, 420, 520,
-    619, 719, 2024, 818, 421, 620, 720, 521, 819, 422, 522, 621, 721, 820, 622, 423, 722, 523, 821, 623, 723, 822,
-    823,
+    2000, 0, 100, 1, 101, 2, 200, 300, 102, 3, 201, 1301, 103, 4, 202, 302, 104, 5, 105, 203, 6, 400, 500, 204, 304,
+    205, 305, 106, 1401, 7, 2001, 402, 502, 206, 306, 1501, 8, 107, 2002, 600, 700, 9, 207, 307, 2003, 602, 702,
+    404, 504, 10, 108, 2004, 11, 405, 505, 208, 308, 1601, 2005, 604, 704, 109, 12, 800, 2006, 209, 309, 13, 605,
+    705, 406, 506, 2007, 110, 2008, 802, 2009, 407, 507, 210, 310, 1303, 14, 1001, 111, 606, 706, 2010, 2011, 804,
+    408, 211, 607, 508, 311, 15, 112, 2012, 707, 805, 409, 509, 2013, 212, 608, 312, 1403, 708, 113, 16, 2014, 806,
+    609, 410, 510, 213, 313, 1101, 17, 114, 2015, 709, 807, 610, 411, 511, 214, 314, 1201, 1503, 2016, 808, 115,
+    710, 412, 512, 2017, 611, 215, 315, 809, 711, 413, 513, 612, 116, 2018, 712, 414, 514, 216, 613, 316, 117, 1603,
+    18, 810, 415, 118, 19, 515, 217, 317, 119, 713, 20, 811, 614, 218, 318, 21, 219, 319, 22, 714, 23, 615, 812,
+    416, 516, 2019, 120, 2020, 2025, 715, 417, 517, 2026, 220, 1003, 320, 2021, 121, 2027, 616, 2028, 813, 221, 321,
+    2029, 418, 617, 518, 122, 716, 814, 222, 322, 717, 419, 815, 519, 123, 618, 718, 223, 323, 816, 1103, 619, 420,
+    520, 719, 2022, 817, 1203, 620, 720, 818, 2023, 421, 521, 819, 422, 522, 621, 721, 820, 2024, 423, 622, 722,
+    523, 821, 623, 723, 822, 823,
 )
 BF = jnp.bfloat16
 F32 = jnp.float32
@@ -362,13 +363,13 @@
 def mega(
     tok_hbm, seg_hbm, pad_hbm, v0, v1, v2, v3, v4, v5, v6, v7, bias_hbm,
     cot_hbm, qkv_hbm, out_hbm, up_hbm, down_hbm,
-    lo_hbm, gt_hbm, qkv_g, out_g, up_g, down_g, small_g,
-    tokens, seg_row, pad_row, seg_key, lines, bias_in, packed, g_qkv, g_out, g_up, g_down, g_small,
-    w_qkv, w_out, w_up, w_down, small, vec, up_bias, tok_t, q_s, k_s, v_s, prob, ctx, ctx_t, hat_s, r_s,
-    low, low_t, part, act_t, gelu_d, big, ra, rb, rc, rd, acc, bias_up_g, sg, sra, srb, src, srd,
+    lo, big, g_qkv, g_out, g_up, g_down, g_small,
+    tokens, seg_row, pad_row, side, lines, bias_in, packed,
+    w_qkv, w_out, w_up, w_down, small, vec, up_bias, tok_t, q_s, k_s, v_s, prob, ctx, ctx_t, hat_s,
+    low, low_t, part, act_t, gelu_d, ra, rb, rc, rd, acc, bias_up_g, sg, sra, srb, src, srd,
     ag_zr, ag_r1, ag_r2, ag_rc, ag_own, ag_s0, ag_s1, ag_s2,
     sa_s, sa_r, sb_s, sb_r, sc_s, sc_r, sd_s, sd_r, sm_s, sm_r, loc, inp,
-    cred_a, cred_b, cred_c, cred_d,
+    cred_a, cred_b, cred_c, cred_d, rab, zb, fb, nb, ba_r, bz_s, bz_r, bf_s, bf_r, bn_s, bn_r,
 ):
     at = Place()
     at.setup()
@@ -475,35 +476,50 @@
     keep = [c * (x * 2 + t) + (1 - c) * (t * 2 + y) for t in (0, 1)]
     away = [c * ((1 - x) * 2 + t) + (1 - c) * (t * 2 + 1 - y) for t in (0, 1)]
     mine = (1 - c) * x + c * y
-    total = 24
+    ring = [k for k in range(24) if k not in ZFIRST]
+    total = len(ring)
 
     def send_a(k):
-        p, a = k % NP, k % NA
-        if k >= NA:
-            pl.semaphore_wait(cred_a, 1)
+        p = k % NP
+        if k in ZFIRST:
+            j = ZFIRST.index(k)
+            land, sem = rab.at[j], ba_r.at[j]
+        else:
+            n = ring.index(k)
+            land, sem = ra.at[n % NA], sa_r.at[n % NA]
+            if n >= NA:
+                pl.semaphore_wait(cred_a, 1)
         for plane in range(4):
-            send(part.at[p, plane, :, 1 - c], ra.at[a, plane], sa_s.at[p], sa_r.at[a], at.twin)
+            send(part.at[p, plane, :, 1 - c], land.at[plane], sa_s.at[p], sem, at.twin)
 
     def add_a(k):
-        p, a = k % NP, k % NA
-        wait_for(ra.at[a], sa_r.at[a])
+        p = k % NP
+        if k in ZFIRST:
+            j = ZFIRST.index(k)
+            land, sem = rab.at[j], ba_r.at[j]
+        else:
+            n = ring.index(k)
+            land, sem = ra.at[n % NA], sa_r.at[n % NA]
+        wait_for(land, sem)
 
         def step(plane):
-            mix = ra[a, plane].astype(F32) + part[p, plane, :, c].astype(F32)
-            ra[a, plane] = mix.astype(BF)
+            mix = land[plane].astype(F32) + part[p, plane, :, c].astype(F32)
+            land[plane] = mix.astype(BF)
 
         loop(4, step)
-        wait_for(ra.at[a], sa_s.at[p])
+        wait_for(land, sa_s.at[p])
 
     def send_b(k):
-        a, b = k % NA, k % NB
-        if k >= NB:
+        n = ring.index(k)
+        a, b = n % NA, n % NB
+        if n >= NB:
             pl.semaphore_wait(cred_b, 1)
         for t in (0, 1):
             send(ra.at[a, :, away[t]], rb.at[b, :, t], sb_s.at[a], sb_r.at[b], at.far)
 
     def add_b(k):
-        a, b = k % NA, k % NB
+        n = ring.index(k)
+        a, b = n % NA, n % NB
         wait_for(rb.at[b], sb_r.at[b])
 
         def step(plane):
@@ -513,17 +529,19 @@
 
         loop(4, step)
         wait_for(rb.at[b], sb_s.at[a])
-        if k + NA < total:
+        if n + NA < total:
             pl.semaphore_signal(cred_a, inc=1, device_id=at.twin, device_id_type=MESH)
 
     def send_c(k):
-        b, cc = k % NB, k % NC
-        if k >= NC:
+        n = ring.index(k)
+        b, cc = n % NB, n % NC
+        if n >= NC:
             pl.semaphore_wait(cred_c, 1)
         send(rb.at[b, :, 1 - mine], rc.at[cc], sc_s.at[b], sc_r.at[cc], at.near)
 
     def add_c(k):
-        b, cc = k % NB, k % NC
+        n = ring.index(k)
+        b, cc = n % NB, n % NC
         wait_for(rc.at[cc], sc_r.at[cc])
 
         def step(plane):
@@ -532,40 +550,64 @@
 
         loop(4, step)
         wait_for(rc.at[cc], sc_s.at[b])
-        if k + NB < total:
+        if n + NB < total:
             pl.semaphore_signal(cred_b, inc=1, device_id=at.far, device_id_type=MESH)
 
     def send_d(k):
-        cc, d = k % NC, k % ND
+        n = ring.index(k)
+        cc, d = n % NC, n % ND
         for o in range(3):
-            if k >= ND:
+            if n >= ND:
                 pl.semaphore_wait(cred_d.at[o], 1)
             send(rc.at[cc, (z + o + 1) % 4], rd.at[d, o], sd_s.at[cc], sd_r.at[d], at.ups[o])
 
-    def target(k, out=False):
+    def send_z(k, square):
+        j = ZFIRST.index(k)
+        for o in range(3):
+            send(rab.at[j, (z + o + 1) % 4, square], zb.at[j, o, square], bz_s.at[j], bz_r.at[j], at.ups[o])
+
+    def add_z(k):
+        j = ZFIRST.index(k)
+        wait_for(zb.at[j], bz_r.at[j])
+        mix = rab[j, z].astype(F32) + zb[j, 0].astype(F32) + zb[j, 1].astype(F32) + zb[j, 2].astype(F32)
+        rab[j, z] = mix.astype(BF)
+        for t in (0, 1):
+            send(rab.at[j, z, away[t]], fb.at[j, t], bf_s.at[j], bf_r.at[j], at.far)
+
+    def add_far(k):
+        j = ZFIRST.index(k)
+        wait_for(fb.at[j], bf_r.at[j])
+        for t in (0, 1):
+            fb[j, t] = (fb[j, t].astype(F32) + rab[j, z, keep[t]].astype(F32)).astype(BF)
+        send(fb.at[j, 1 - mine], nb.at[j], bn_s.at[j], bn_r.at[j], at.near)
+
+    def add_near(k):
+        j = ZFIRST.index(k)
+        wait_for(nb.at[j], bn_r.at[j])
+        put_out(k, fb[j, mine].astype(F32) + nb[j].astype(F32))
+        wait_for(zb.at[j], bz_s.at[j])
+        wait_for(fb.at[j], bf_s.at[j])
+        wait_for(nb.at[j], bn_s.at[j])
+
+    def put_out(k, value):
         if k < 8:
-            pick = (pl.ds(32 * (k // 2), 32), pl.ds(CW * (k % 2), CW))
+            g_down[pl.ds(32 * (k // 2), 32), pl.ds(CW * (k % 2), CW)] = value
         elif k < 16:
-            pick = (slice(None), pl.ds(CW * (k - 8), CW))
+            g_up[:, pl.ds(CW * (k - 8), CW)] = value
         elif k < 18:
-            pick = (slice(None), pl.ds(CW * (k - 16), CW))
+            g_out[:, pl.ds(CW * (k - 16), CW)] = value
         else:
-            pick = (slice(None), pl.ds(CW * (k - 18), CW))
-        which = (k >= 8) + (k >= 16) + (k >= 18)
-        ref = (g_down, g_up, g_out, g_qkv)[which].at[pick]
-        return (ref, (down_g, up_g, out_g, qkv_g)[which].at[pick], 2 + which) if out else ref
+            g_qkv[:, pl.ds(CW * (k - 18), CW)] = value
 
     def add_d(k):
-        cc, d = k % NC, k % ND
+        n = ring.index(k)
+        cc, d = n % NC, n % ND
         wait_for(rd.at[d], sd_r.at[d])
-        mix = rc[cc, z].astype(F32) + rd[d, 0].astype(F32) + rd[d, 1].astype(F32) + rd[d, 2].astype(F32)
-        target(k)[...] = mix
-        source, dest, index = target(k, True)
-        pltpu.make_async_copy(source, dest, loc.at[index]).start()
+        put_out(k, rc[cc, z].astype(F32) + rd[d, 0].astype(F32) + rd[d, 1].astype(F32) + rd[d, 2].astype(F32))
         wait_for(rd.at[d], sd_s.at[cc])
-        if k + NC < total:
+        if n + NC < total:
             pl.semaphore_signal(cred_c, inc=1, device_id=at.near, device_id_type=MESH)
-        if k + ND < total:
+        if n + ND < total:
             for o in range(3):
                 pl.semaphore_signal(cred_d.at[o], inc=1, device_id=at.downs[o], device_id_type=MESH)
 
@@ -605,7 +647,7 @@
         r, l = ds(block * SPAN, SPAN), ds(pair * LANES, LANES)
         queries, key_rows, values_t = q_s[r, l], k_s[r, l], v_s[r, l].T
         diagonal = lax.broadcasted_iota(jnp.int32, (SPAN, SPAN), 0) == lax.broadcasted_iota(jnp.int32, (SPAN, SPAN), 1)
-        allowed = (seg_key[r, :] == seg_row[:, r].astype(F32)) | diagonal
+        allowed = (side[r, 0:1] == seg_row[:, r].astype(F32)) | diagonal
         halves = []
         for high in (0, 1):
             scores = nt(split(key_rows, high), queries) * scale
@@ -662,7 +704,7 @@
             r = ds(n * ROWS, ROWS)
             hat, inverse = norm_stats(big[r, :])
             hat_s[r, :] = hat
-            r_s[r, :] = inverse
+            side[r, 1:2] = inverse
             normed = hat * vec[3:4, :] + vec[4:5, :]
             low[r, :] = normed.astype(BF)
             big[r, :] = normed + vec[5:6, :]
@@ -696,8 +738,8 @@
         def step(n):
             r = ds(n * ROWS, ROWS)
             hat, inverse = norm_stats(big[r, :])
-            cot = ctx[r, :].astype(F32)
-            ctx[r, :] = (hat * vec[6:7, :] + vec[7:8, :]).astype(BF)
+            cot = lo[r, :].astype(F32)
+            lo[r, :] = (hat * vec[6:7, :] + vec[7:8, :]).astype(BF)
             acc[0] += folded(cot * hat)
             acc[1] += folded(cot)
             scaled = cot * vec[6:7, :]
@@ -718,7 +760,7 @@
             acc[3] += folded(incoming * hat)
             acc[4] += folded(incoming)
             scaled = incoming * vec[3:4, :]
-            grad = r_s[r, :] * (
+            grad = side[r, 1:2] * (
                 scaled - jnp.mean(scaled, -1, keepdims=True) - hat * jnp.mean(scaled * hat, -1, keepdims=True)
             )
             big[r, :] = grad
@@ -803,7 +845,7 @@
         for n in range(rows // LANES):
             r = slice(LANES * n, LANES * (n + 1))
             key = jnp.where(pad_row[:, r] == 1, seg_row[:, r], -1).astype(F32)
-            seg_key[r, :] = jnp.broadcast_to(key, (LANES, LANES)).T[:, 0:1]
+            side[r, 0:1] = jnp.broadcast_to(key, (LANES, LANES)).T[:, 0:1]
         transpose_rows(tokens, tok_t)
 
     def unpack():
@@ -816,7 +858,7 @@
             up_bias[:, LANES * j:LANES * (j + 1)] = small[j // 8, (j % 8) // 2, j % 2].astype(F32)[8:9]
 
     def norm_first():
-        pltpu.make_async_copy(cot_hbm, ctx, loc.at[0]).start()
+        pltpu.make_async_copy(cot_hbm, lo, loc).start()
         norm_one()
 
     units = blocks * pairs
@@ -833,7 +875,7 @@
         else:
             forward[code - 600]()
 
-    pltpu.make_async_copy(cot_hbm, ctx, loc.at[0]).wait()
+    pltpu.make_async_copy(cot_hbm, lo, loc).wait()
 
     def small_grads():
         for row in range(6):
@@ -877,32 +919,21 @@
         wait_for(srd, sm_r.at[3])
         g_small[...] = src[z] + srd[0] + srd[1] + srd[2]
         g_small[0:8] = pltpu.roll(g_small[0:8], (4 - place) % 4 * 32, 1)
-        pltpu.make_async_copy(g_small, small_g, loc.at[6]).start()
         wait_for(sra, sm_s.at[0])
         wait_for(srb, sm_s.at[1])
         wait_for(src, sm_s.at[2])
         wait_for(srd, sm_s.at[3])
 
-    def finish_norm():
-        norm_two()
-        pltpu.make_async_copy(ctx, lo_hbm, loc.at[1]).start()
-
-    def to_context():
-        pltpu.make_async_copy(ctx, lo_hbm, loc.at[1]).wait()
-        context_back()
-
-    def write_tokens():
-        pltpu.make_async_copy(big, gt_hbm, loc.at[0]).start()
-
-    backward = [finish_norm]
+    backward = [norm_two]
     backward += [lambda i=i: up_back(2 * i, 2) for i in range(8)]
     backward += [lambda i=i: normed_back(i) for i in range(4)]
-    backward += [norm_one_back, to_context]
+    backward += [norm_one_back, context_back]
     backward += [lambda i=i: loop(units // 4, lambda u: attend_back(u + i * (units // 4))) for i in range(4)]
     backward += [small_grads, small_a, small_b, small_c, small_d, small_e]
     backward += [lambda i=i: token_back(i) for i in range(4)]
-    backward += [write_tokens]
-    stages = (produce, send_a, add_a, send_b, add_b, send_c, add_c, send_d, add_d)
+    backward += [lambda: None]
+    stages = (produce, send_a, add_a, send_b, add_b, send_c, add_c, send_d, add_d, None, add_z, add_far, add_near)
+    stages += tuple(lambda k, square=square: send_z(k, square) for square in range(4))
     for code in BACKWARD:
         if code < 2000:
             stages[code // 100](code % 100)
@@ -911,38 +942,18 @@
 
     for k in range(count):
         gather_end(k)
-    pltpu.make_async_copy(big, gt_hbm, loc.at[0]).wait()
-    for index, (source, dest) in enumerate(((g_down, down_g), (g_up, up_g), (g_out, out_g), (g_qkv, qkv_g), (g_small, small_g))):
-        pltpu.make_async_copy(source, dest, loc.at[2 + index]).wait()
-
-
-def finish(
-    lo, gt, qkv, out, up, down, small,
-    lo_o, gt_o, qkv_o, out_o, up_o, down_o, s0, s1, s2, s3, s4, s5, s6, s7, s8,
-    lo_v, gt_v, qkv_v, out_v, up_v, down_v, sem_in, sem_out,
-):
-    moves = []
-    for src, mid, dst, parts in (
-        (gt, gt_v, gt_o, 4), (lo, lo_v, lo_o, 2), (up, up_v, up_o, 1), (down, down_v, down_o, 1), (qkv, qkv_v, qkv_o, 1),
-        (out, out_v, out_o, 1),
-    ):
-        size = src.shape[0] // parts
-        for i in range(parts):
-            r, n = pl.ds(i * size, size), len(moves)
-            moves.append((
-                pltpu.make_async_copy(src.at[r], mid.at[r], sem_in.at[n]),
-                pltpu.make_async_copy(mid.at[r], dst.at[r], sem_out.at[n]),
-            ))
-    for take, _ in moves:
-        take.start()
-    for i, ref in enumerate((s0, s1, s2, s3, s4, s5, s6, s7)):
-        ref[...] = small[i:i + 1, 0:32]
-    s8[...] = small[8:9, :]
-    for take, put in moves:
-        take.wait()
-        put.start()
-    for _, put in moves:
-        put.wait()
+
+
+def finish(*refs):
+    sources, small, targets, lines, sem = refs[:6], refs[6], refs[7:13], refs[13:22], refs[22]
+    copies = [pltpu.make_async_copy(a, b, sem.at[i]) for i, (a, b) in enumerate(zip(sources, targets))]
+    for copy in copies:
+        copy.start()
+    for i in range(8):
+        lines[i][...] = small[i:i + 1, 0:32]
+    lines[8][...] = small[8:9, :]
+    for copy in copies:
+        copy.wait()
 
 
 def fused(
@@ -959,17 +970,17 @@
     blocks = rows // SPAN
     count = 25
     dma = pltpu.SemaphoreType.DMA
-    own_shapes = [w.shape for w in (w_qkv, w_out, w_up, w_down)]
+    arrays = [jax.ShapeDtypeStruct((rows, width), BF), jax.ShapeDtypeStruct((rows, width), F32)]
+    arrays += [jax.ShapeDtypeStruct(w.shape, F32) for w in (w_qkv, w_out, w_up, w_down)]
     scratch = [
         pltpu.VMEM((rows, width), BF),
         pltpu.VMEM((1, rows), jnp.int32),
         pltpu.VMEM((1, rows), jnp.int32),
-        pltpu.VMEM((rows, 1), F32),
+        pltpu.VMEM((rows, 2), F32),
         pltpu.VMEM((8, 1, 32), BF),
         pltpu.VMEM((1, LANES), BF),
         pltpu.VMEM((16, LANES), BF),
     ]
-    scratch += [pltpu.VMEM(shape, F32) for shape in own_shapes] + [pltpu.VMEM((16, LANES), F32)]
     scratch += [
         pltpu.VMEM((4, 4, 2, 32, 3 * width), BF),
         pltpu.VMEM((4, 4, 2, 32, width), BF),
@@ -986,13 +997,11 @@
         pltpu.VMEM((rows, width), BF),
         pltpu.VMEM((width, rows), BF),
         pltpu.VMEM((rows, width), F32),
-        pltpu.VMEM((rows, 1), F32),
         pltpu.VMEM((rows, width), BF),
         pltpu.VMEM((width, rows), BF),
         pltpu.VMEM((NP, 4, 4, 2, 32, CW), BF),
         pltpu.VMEM((ff // LANES, LANES, rows), BF),
         pltpu.VMEM((rows, ff), BF),
-        pltpu.VMEM((rows, width), F32),
         pltpu.VMEM((NA, 4, 4, 32, CW), BF),
         pltpu.VMEM((NB, 4, 2, 32, CW), BF),
         pltpu.VMEM((NC, 4, 32, CW), BF),
@@ -1008,42 +1017,40 @@
     scratch += [dma((count,))] * 8
     scratch += [
         dma((NP,)), dma((NA,)), dma((NA,)), dma((NB,)), dma((NB,)), dma((NC,)), dma((NC,)), dma((ND,)),
-        dma((4,)), dma((4,)), dma((7,)), dma((12,)),
+        dma((4,)), dma((4,)), dma, dma((12,)),
         pltpu.SemaphoreType.REGULAR, pltpu.SemaphoreType.REGULAR, pltpu.SemaphoreType.REGULAR,
         pltpu.SemaphoreType.REGULAR((3,)),
     ]
-    result, grad_tokens, g_qkv, g_out, g_up, g_down, g_small = pl.pallas_call(
+    early = len(ZFIRST)
+    scratch += [
+        pltpu.VMEM((early, 4, 4, 32, CW), BF),
+        pltpu.VMEM((early, 3, 4, 32, CW), BF),
+        pltpu.VMEM((early, 2, 32, CW), BF),
+        pltpu.VMEM((early, 32, CW), BF),
+    ]
+    scratch += [dma((early,))] * 7
+    *middle, g_small = pl.pallas_call(
         mega,
-        out_shape=(
-            jax.ShapeDtypeStruct((rows, width), BF),
-            jax.ShapeDtypeStruct((rows, width), F32),
-            jax.ShapeDtypeStruct(w_qkv.shape, F32),
-            jax.ShapeDtypeStruct(w_out.shape, F32),
-            jax.ShapeDtypeStruct(w_up.shape, F32),
-            jax.ShapeDtypeStruct(w_down.shape, F32),
-            jax.ShapeDtypeStruct((16, LANES), F32),
-        ),
+        out_shape=[pltpu.VMEM(a.shape, a.dtype) for a in arrays] + [pltpu.VMEM((16, LANES), F32)],
         in_specs=[anyw] * 17,
-        out_specs=[anyw] * 7,
+        out_specs=[vmem] * 7,
         scratch_shapes=scratch,
         compiler_params=pltpu.CompilerParams(
-            collective_id=0, has_side_effects=True, vmem_limit_bytes=67043328
+            collective_id=0, has_side_effects=True, vmem_limit_bytes=62270000
         ),
         name="layer",
     )(
         tokens, segment_ids.reshape(1, rows), pad_mask.reshape(1, rows), *vectors, cotangent, w_qkv, w_out, w_up, w_down
     )
-    arrays = (result, grad_tokens, g_qkv, g_out, g_up, g_down)
     moved = pl.pallas_call(
         finish,
-        out_shape=[jax.ShapeDtypeStruct(a.shape, a.dtype) for a in arrays]
-        + [jax.ShapeDtypeStruct((1, 32), F32)] * 8 + [jax.ShapeDtypeStruct((1, LANES), F32)],
+        out_shape=arrays + [jax.ShapeDtypeStruct((1, 32), F32)] * 8 + [jax.ShapeDtypeStruct((1, LANES), F32)],
         in_specs=[anyw] * 6 + [vmem],
         out_specs=[anyw] * 6 + [vmem] * 9,
-        scratch_shapes=[pltpu.VMEM(a.shape, a.dtype) for a in arrays] + [dma((10,))] * 2,
-        compiler_params=pltpu.CompilerParams(vmem_limit_bytes=67043328),
+        scratch_shapes=[dma((6,))],
+        compiler_params=pltpu.CompilerParams(vmem_limit_bytes=8388608),
         name="finish",
-    )(*arrays, g_small)
+    )(*middle, g_small)
     result, grad_tokens, g_qkv, g_out, g_up, g_down = moved[:6]
     own = [m.reshape(m.shape[1]) for m in moved[6:]]
     return (

time: 246 us -> 237 us (0.963)
  Pallas kernels: 245 us -> 236 us
    pallas_call x2, Pallas kernels: 245 us -> 236 us  [the longest x1 234 us: fused(): pl.pallas_call(mega, out_shape=[pltpu.VMEM(a.shape, a.dtype) for a in arr...]
where the time goes in v1:
time: 237 us
  Pallas kernels  236 us (100%)
    pallas_call x1, Pallas kernels, fused(): pl.pallas_call(mega, out_shape=[pltpu.VMEM(a.shape, a.dtype) for a in arr...  234 us

profile of v1, /device:TPU:0, one launch (start us, length us, event | category | flops | bytes accessed | tf_op | source)
XLA Modules:
  0.0 237.3 jit_solution(14828285160507173263)
XLA Ops:
  0.7 233.7 %layer.1 = (bf16[512,1024]{1,0:T(8,128)(2,1)S(1)}, f32[512,1024]{1,0:T(8,128)S(1)}, f32[32,3072]{1,0:T(8,128)S(1)}, f32[32,1024]{1,0:T(8,128)S(1)}, f32[32,4096]...) custom-call(bf16[512,1024]{1,0:T(8,128)(2,1)} %tok_hbm.1, s32[1,512]{1,0:T(1,128)} %bitcast.20, ...), custom_call_target="tpu_custom_call" | custom-call | tf_op jit(solution)/shard_map/layer/pallas_call | solution.py:1032
  234.4 2.8 %finish.1 = (bf16[512,1024]{1,0:T(8,128)(2,1)}, f32[512,1024]{1,0:T(8,128)}, f32[32,3072]{1,0:T(8,128)}, f32[32,1024]{1,0:T(8,128)}, f32[32,4096]{1,0:T(8,128)},...) custom-call(bf16[512,1024]{1,0:T(8,128)(2,1)S(1)} %get-tuple-element, ...), custom_call_target="tpu_custom_call" | custom-call | tf_op jit(solution)/shard_map/finish/pallas_call | solution.py:1045

commit v2 on v1

--- a/solution.py
+++ b/solution.py
@@ -275,16 +275,25 @@
     )
 
 
-LATE = (23, 24,)
+PIECES = (
+    (0, 0, 32, 0, 128), (0, 0, 32, 128, 128), (0, 0, 32, 256, 256), (0, 0, 32, 512, 512), (0, 0, 32, 1024, 512), (0,
+    0, 32, 1536, 512), (0, 0, 32, 2048, 512), (0, 0, 32, 2560, 512), (1, 0, 32, 0, 512), (1, 0, 32, 512, 512), (2,
+    0, 32, 0, 512), (2, 0, 32, 512, 512), (2, 0, 32, 1024, 512), (2, 0, 32, 1536, 512), (2, 0, 32, 2048, 512), (2,
+    0, 32, 2560, 512), (2, 0, 32, 3072, 512), (2, 0, 32, 3584, 512), (3, 0, 128, 0, 128), (3, 0, 128, 128, 128), (3,
+    0, 128, 256, 128), (3, 0, 128, 384, 128), (3, 0, 128, 512, 128), (3, 0, 128, 640, 128), (3, 0, 128, 768, 128),
+    (3, 0, 128, 896, 128),
+)
+LATE = (25, 26,)
 ZFIRST = (1, 3,)
 FORWARD = (
-    123, 124, 100, 101, 102, 103, 104, 105, 106, 107, 108, 109, 110, 111, 112, 113, 114, 115, 116, 117, 118, 119,
-    120, 121, 122, 600, 223, 224, 200, 323, 324, 300, 201, 400, 500, 601, 202, 301, 203, 302, 401, 501, 602, 204,
-    303, 402, 205, 502, 603, 304, 403, 206, 305, 503, 604, 207, 404, 306, 504, 605, 208, 307, 405, 505, 606, 209,
-    308, 406, 506, 607, 608, 407, 309, 210, 609, 507, 408, 211, 610, 508, 409, 310, 212, 611, 509, 311, 213, 612,
-    410, 312, 214, 613, 510, 215, 614, 615, 313, 616, 411, 216, 314, 511, 617, 315, 217, 412, 512, 618, 316, 218,
-    317, 219, 318, 413, 513, 619, 220, 319, 414, 221, 514, 620, 415, 320, 222, 515, 621, 321, 416, 322, 516, 622,
-    417, 423, 517, 523, 418, 518, 623, 419, 519, 420, 424, 520, 624, 421, 524, 422, 521, 522, 625, 626,
+    125, 126, 100, 101, 102, 103, 104, 105, 106, 107, 108, 109, 600, 225, 226, 200, 110, 201, 111, 202, 112, 300,
+    301, 203, 113, 302, 400, 500, 601, 401, 303, 402, 501, 204, 114, 502, 403, 205, 115, 304, 503, 602, 206, 116,
+    305, 404, 207, 117, 504, 603, 306, 405, 208, 118, 307, 505, 604, 209, 119, 406, 308, 506, 605, 210, 120, 309,
+    407, 507, 606, 211, 121, 310, 408, 212, 122, 325, 508, 607, 311, 608, 409, 312, 213, 123, 609, 509, 410, 214,
+    124, 610, 510, 313, 215, 611, 411, 314, 216, 326, 612, 511, 412, 315, 613, 512, 217, 614, 615, 316, 616, 413,
+    218, 513, 617, 317, 219, 414, 318, 514, 618, 220, 319, 415, 515, 619, 221, 320, 416, 516, 620, 222, 321, 417,
+    517, 621, 322, 418, 518, 622, 425, 419, 223, 525, 519, 420, 224, 520, 623, 323, 324, 421, 521, 422, 522, 624,
+    426, 423, 526, 523, 424, 524, 625, 626,
 )
 BACKWARD = (
     2000, 0, 100, 1, 101, 2, 200, 300, 102, 3, 201, 1301, 103, 4, 202, 302, 104, 5, 105, 203, 6, 400, 500, 204, 304,
@@ -384,14 +393,15 @@
             src_ref=src, dst_ref=dst, send_sem=s, recv_sem=r, device_id=device, device_id_type=MESH
         ).start()
 
-    pieces = [(packed, small, 0, LANES)]
-    for hbm, full, wide in ((qkv_hbm, w_qkv, CW), (out_hbm, w_out, CW), (up_hbm, w_up, CW), (down_hbm, w_down, LANES)):
-        pieces += [(hbm, full, start, wide) for start in range(0, hbm.shape[1], wide)]
+    pieces = [(packed, small, (pl.ds(0, 16), pl.ds(0, LANES)))]
+    for which, first, deep, start, wide in PIECES:
+        hbm, full = ((qkv_hbm, w_qkv), (out_hbm, w_out), (up_hbm, w_up), (down_hbm, w_down))[which]
+        pieces.append((hbm, full, (pl.ds(first, deep), pl.ds(start, wide))))
     count = len(pieces)
 
     def spot(k, plane, square, core):
-        _, full, start, wide = pieces[k]
-        return full.at[plane, square, core, :, pl.ds(start, wide)]
+        _, full, cut = pieces[k]
+        return full.at[(plane, square, core) + cut]
 
     every = slice(None)
     barrier = pltpu.get_barrier_semaphore()
@@ -427,8 +437,8 @@
     b_ups = [(peer, ag_s1, ag_zr) for peer in at.ups]
 
     def own_piece(k):
-        hbm, _, start, wide = pieces[k]
-        return hbm.at[:, pl.ds(start, wide)]
+        hbm, _, cut = pieces[k]
+        return hbm.at[cut]
 
     def gather_1(k):
         block = spot(k, z, own, c)
@@ -968,7 +978,7 @@
     anyw = pl.BlockSpec(memory_space=pl.ANY)
     pairs = width // LANES
     blocks = rows // SPAN
-    count = 25
+    count = len(PIECES) + 1
     dma = pltpu.SemaphoreType.DMA
     arrays = [jax.ShapeDtypeStruct((rows, width), BF), jax.ShapeDtypeStruct((rows, width), F32)]
     arrays += [jax.ShapeDtypeStruct(w.shape, F32) for w in (w_qkv, w_out, w_up, w_down)]

time: 237 us -> 236 us (level)
  no operation moved by 1% of the time
where the time goes in v2:
time: 236 us
  Pallas kernels  235 us (100%)
    pallas_call x1, Pallas kernels, fused(): pl.pallas_call(mega, out_shape=[pltpu.VMEM(a.shape, a.dtype) for a in arr...  232 us

profile of v2, /device:TPU:0, one launch (start us, length us, event | category | flops | bytes accessed | tf_op | source)
XLA Modules:
  0.0 236.0 jit_solution(2358694039043023151)
XLA Ops:
  0.7 232.4 %layer.1 = (bf16[512,1024]{1,0:T(8,128)(2,1)S(1)}, f32[512,1024]{1,0:T(8,128)S(1)}, f32[32,3072]{1,0:T(8,128)S(1)}, f32[32,1024]{1,0:T(8,128)S(1)}, f32[32,4096]...) custom-call(bf16[512,1024]{1,0:T(8,128)(2,1)} %tok_hbm.1, s32[1,512]{1,0:T(1,128)} %bitcast.20, ...), custom_call_target="tpu_custom_call" | custom-call | tf_op jit(solution)/shard_map/layer/pallas_call | solution.py:1042
  233.0 2.8 %finish.1 = (bf16[512,1024]{1,0:T(8,128)(2,1)}, f32[512,1024]{1,0:T(8,128)}, f32[32,3072]{1,0:T(8,128)}, f32[32,1024]{1,0:T(8,128)}, f32[32,4096]{1,0:T(8,128)},...) custom-call(bf16[512,1024]{1,0:T(8,128)(2,1)S(1)} %get-tuple-element, ...), custom_call_target="tpu_custom_call" | custom-call | tf_op jit(solution)/shard_map/finish/pallas_call | solution.py:1055
